TPU v7x, 128 devices: a whole 4x4x4 slice. The times are simulated.
128 devices in a mesh: kring: 8 (over y, x_lo), band: 16 (over z, x_hi, core).
Axes of the slice: x: 4 (x_hi: 2, x_lo: 2; x = x_hi * 2 + x_lo), y: 4, z: 4, core: 2. Of those that a mesh axis runs over, the one named last changes fastest.
Arguments:
- current: bfloat16 [262144, 256], P(('kring', 'band')), may hold values from -61 to 61
- previous: bfloat16 [262144, 256], P(('kring', 'band')), may hold values from -6 to 6
- energies: float32 [262144], P(('kring', 'band')), may hold values from 1.5 to 2.5
- targets: int32 [262144], P(('kring', 'band')), may hold values from 0 to 15, as said below
- layer_ids: int32 [327680], P(('kring', 'band')), may hold values from 0 to 1
- conduction_pairs: bfloat16 [327680, 1024], P(('kring', 'band')), may hold values from -0.375 to 0.375
- valence_pairs: bfloat16 [327680, 1024], P(('kring', 'band')), may hold values from -0.228125 to 0.228125
- exchange_pairs: bfloat16 [327680, 1024], P(('kring', 'band')), may hold values from -0.137001939 to 0.137001939
- screened: bfloat16 [8, 2, 1024, 2, 1024], P(None, None, 'band'), may hold values from -0.03203125 to 1.28203125
- coulomb: float32 [2, 2, 1024], replicated, may hold values from 0.2 to 2
- beta_prev: float32 [256], replicated, may hold values from 0.5 to 2
Outputs:
- next_vector: bfloat16 [262144, 256], P(('kring', 'band'))
- lanczos_alpha: float32 [256], replicated
- lanczos_beta: float32 [256], replicated
Inputs may be any that keep to these rules, and one draw needn't show every extreme that they name: `targets`: the 2048 rows of one device name each band index at most 2560 // 16 times; in every k-group one band index is named exactly that often by every device of the group.
All inputs are finite; a program needn't handle non-finite values.
Results may differ from a plain program's by a relative error of at most 0.0057.
Values may be sent and summed in bfloat16 or wider, within the bound.
A program may use at most 128 MiB of HBM per device.

v0:
```python
import jax
import jax.numpy as jnp
from jax import lax
from jax.sharding import PartitionSpec as P

epsilon_mean = 1e-06


def place_rows(targets, capacity, band_count):
    onehot = (targets[:, None] == jnp.arange(band_count, dtype=jnp.int32)[None, :]).astype(
        jnp.int32
    )
    counted = jnp.cumsum(onehot, axis=0)
    ranking = jnp.sum(counted * onehot, axis=1) - 1
    return targets * capacity + ranking


def per_device(
    current,
    previous,
    energies,
    targets,
    layer_ids,
    conduction_pairs,
    valence_pairs,
    exchange_pairs,
    screened,
    coulomb,
    beta_prev,
):
    band_count = lax.axis_size("band")
    own_rows, chains = current.shape
    slot_rows, basis_size = conduction_pairs.shape
    capacity = slot_rows // band_count
    slot_ids = place_rows(targets, capacity, band_count)
    outgoing = jnp.zeros((slot_rows, chains), jnp.bfloat16).at[slot_ids].set(current)
    arrived = lax.all_to_all(
        outgoing.reshape(band_count, capacity, chains),
        "band",
        split_axis=0,
        concat_axis=0,
        tiled=True,
    ).reshape(slot_rows, chains)
    layer_pick = (layer_ids[:, None] == jnp.arange(2, dtype=jnp.int32)[None, :]).astype(
        jnp.bfloat16
    )
    split_amps = arrived[:, None, :] * layer_pick[:, :, None]
    valence_part = jnp.einsum(
        "tg,tln->lgn", valence_pairs, split_amps, preferred_element_type=jnp.float32
    )
    exchange_part = jnp.einsum(
        "tg,tln->lgn", exchange_pairs, split_amps, preferred_element_type=jnp.float32
    )
    projected = lax.psum_scatter(valence_part, "band", scatter_dimension=1, tiled=True).astype(
        jnp.bfloat16
    )
    exchange_total = lax.psum(exchange_part, ("kring", "band"))
    coupled = (
        coulomb[:, 0, :, None] * exchange_total[0][None]
        + coulomb[:, 1, :, None] * exchange_total[1][None]
    ).astype(jnp.bfloat16)
    group_index = lax.axis_index("kring")
    group_count = lax.axis_size("kring")
    pieces = lax.all_gather(projected[None], "kring", axis=0, tiled=True)
    number = pieces.shape[0]
    distance = jnp.mod(group_index - jnp.arange(number, dtype=jnp.int32), group_count)
    blocks = jnp.take(screened, distance, axis=0)
    direct_part = jnp.einsum("kaphg,kapn->hgn", blocks, pieces, preferred_element_type=jnp.float32)
    direct = lax.psum(direct_part, "band").astype(jnp.bfloat16)
    both_direct = jnp.einsum(
        "tg,lgn->tln", conduction_pairs, direct, preferred_element_type=jnp.float32
    )
    both_exchange = jnp.einsum(
        "tg,lgn->tln", exchange_pairs, coupled, preferred_element_type=jnp.float32
    )
    kernel_all = 2.0 * both_exchange - both_direct
    kernel_rows = jnp.sum(kernel_all * layer_pick.astype(jnp.float32)[:, :, None], axis=1).astype(
        jnp.bfloat16
    )
    returned = lax.all_to_all(
        kernel_rows.reshape(band_count, capacity, chains),
        "band",
        split_axis=0,
        concat_axis=0,
        tiled=True,
    ).reshape(slot_rows, chains)
    kernel_own = returned[slot_ids].astype(jnp.float32)
    current_wide = current.astype(jnp.float32)
    applied = energies[:, None] * current_wide + kernel_own
    start_vec = applied - beta_prev[None, :] * previous.astype(jnp.float32)
    total_rows = own_rows * group_count * band_count
    projection, self_norm = lax.psum(
        (jnp.sum(current_wide * start_vec, axis=0), jnp.sum(current_wide * current_wide, axis=0)),
        ("kring", "band"),
    )
    lanczos_alpha = projection / self_norm
    residual = start_vec - lanczos_alpha[None, :] * current_wide
    residual_sq = lax.psum(jnp.sum(residual * residual, axis=0), ("kring", "band"))
    lanczos_beta = jnp.sqrt(residual_sq / total_rows + epsilon_mean)
    next_vector = (residual / lanczos_beta[None, :]).astype(jnp.bfloat16)
    return (next_vector, lanczos_alpha, lanczos_beta)


def solution(mesh):
    in_specs = (
        P(("kring", "band"), None),
        P(("kring", "band"), None),
        P(("kring", "band")),
        P(("kring", "band")),
        P(("kring", "band")),
        P(("kring", "band"), None),
        P(("kring", "band"), None),
        P(("kring", "band"), None),
        P(None, None, "band", None, None),
        P(),
        P(),
    )
    out_specs = (P(("kring", "band"), None), P(), P())
    return jax.shard_map(
        per_device, mesh=mesh, in_specs=in_specs, out_specs=out_specs, check_vma=False
    )
```

profile of v0, /device:TPU:1, one launch (start us, length us, event | category | flops | bytes accessed | tf_op | source)
XLA Modules:
  0.0 529.2 jit_solution(18126593749929816699)
XLA Ops:
  7.9 4.5 reduce-window.6
  14.7 10.8 %scatter_custom_fusion = bf16[2560,256]{1,0:T(8,128)(2,1)} fusion(s32[2048]{0:T(1024)S(1)} %get-tuple-element.8, bf16[2048,256]{1,0:T(8,128)(2,1)} %param.11, bf16[]{:T(256)} %constant.46.clone.1), kind=kCustom, calls=%fused_computation.44 | custom fusion | bytes 1311232 | tf_op jit(solution)/shard_map/scatter | solution.py:36
  25.5 9.3 %all-to-all-start = ((bf16[16,160,256]{2,1,0:T(8,128)(2,1)}), bf16[16,160,256]{2,1,0:T(8,128)(2,1)S(1)}, u32[]{:S(2)}, u32[]{:S(2)}) async-start(bf16[16,160,256]{2,1,0:T(8,128)(2,1)} %bitcast.2), calls=%async_computation | async-start | bytes 2621440 | tf_op jit(solution)/shard_map/all_to_all | solution.py:37
  36.4 12.0 %gather_fusion = bf16[8,2,64,2,1024]{4,3,2,1,0:T(2,128)(2,1)} fusion(bf16[8,2,64,2,1024]{4,3,2,1,0:T(2,128)(2,1)} %param.19, s32[1024]{0:T(1024)S(1)} %pad_clamp_fusion), kind=kCustom, calls=%fused_computation | custom fusion | bytes 8388640 | tf_op jit(solution)/shard_map/jit(_take)/gather | solution.py:67
  48.4 7.8 %broadcast_select_fusion = bf16[8,2,64,2,1024]{4,3,2,1,0:T(2,128)(2,1)} fusion(bf16[8,2,64,2,1024]{4,3,2,1,0:T(2,128)(2,1)} %gather_fusion, pred[8]{0:T(512)(128)(4,1)S(1)} %compare_and_fusion), kind=kLoop, calls=%fused_computation.3 | loop fusion | flops 2097152 | bytes 8388616 | tf_op jit(solution)/shard_map/jit(_take)/select_n | solution.py:67
  57.0 6.7 %fusion.28 = f32[2,1024,256]{1,2,0:T(8,128)} fusion(bf16[2560,1024]{1,0:T(8,128)(2,1)} %param.17, bf16[2560,2]{0,1:T(2,128)(2,1)S(1)} %get-tuple-element.10, bf16[2560,256]{0,1:T(8,128)(2,1)S(1)} %copy.21), kind=kOutput, calls=%fused_computation.32 | convolution fusion | flops 2685665280 | bytes 8660992 | tf_op jit(solution)/shard_map/tg,tln->lgn/dot_general | solution.py:48
  63.6 2.8 copy.22
  66.5 84.6 %all-reduce.7 = bf16[2,1024,256]{2,0,1:T(2,128)(2,1)} all-reduce(f32[2,1024,256]{2,0,1:T(2,128)S(1)} %copy.22), channel_id=3, replica_groups=mesh['kring'=8,'band'=16] {'band'}, use_global_device_ids=true, to_apply=%region_5.6.clone | all-reduce | flops 524288 | bytes 3145728
  151.1 0.9 dynamic-slice_convert_fusion
  152.0 25.1 %all-gather = bf16[16,64,256]{2,1,0:T(8,128)(2,1)S(1)} all-gather(bf16[2,64,256]{2,1,0:T(8,128)(2,1)S(1)} %copy.23), channel_id=2, replica_groups=mesh['kring'=8,'band'=16] {'kring'}, dimensions={0}, use_global_device_ids=true | all-gather | bytes 589824 | tf_op jit(solution)/shard_map/all_gather | solution.py:64
  177.1 4.3 fusion.20
  181.4 4.3 fusion.23
  185.7 91.2 %all-reduce.8 = bf16[2,1024,256]{2,1,0:T(8,128)(2,1)S(1)} all-reduce(f32[2,1024,256]{2,1,0:T(8,128)S(1)} %fusion.20), channel_id=1, replica_groups=mesh['kring'=8,'band'=16] {'band'}, use_global_device_ids=true, to_apply=%region_6.7 | all-reduce | flops 524288 | bytes 3145728 | tf_op jit(solution)/shard_map/psum | solution.py:69
  277.0 7.3 %fusion.1 = f32[2,256,2560]{2,1,0:T(8,128)} fusion(bf16[2560,1024]{1,0:T(8,128)(2,1)} %param.16, bf16[2,1024,256]{2,1,0:T(8,128)(2,1)S(1)} %all-reduce.8), kind=kOutput, calls=%fused_computation.6 | convolution fusion | flops 2684354560 | bytes 11534336 | tf_op jit(solution)/shard_map/tg,lgn->tln/dot_general | solution.py:70
  284.3 64.9 %all-reduce.6.cloned.1.call-done = f32[2,1024,256]{1,2,0:T(8,128)} async-done(((f32[2,1024,256]{1,2,0:T(8,128)}), f32[2,1024,256]{1,2,0:T(8,128)}) %all-reduce.6.cloned.1.call-update) | async-done | bytes 2097168 | tf_op jit(solution)/shard_map/psum | solution.py:57
  349.2 1.7 slice_bitcast_fusion.1
  350.9 6.9 %fusion = bf16[2560,256]{0,1:T(8,128)(2,1)S(1)} fusion(f32[2,256,2560]{2,1,0:T(8,128)} %fusion.1, bf16[2560,1024]{1,0:T(8,128)(2,1)} %param.18, f32[2560,2]{0,1:T(2,128)S(1)} %get-tuple-element.9, f32[1024,256]{0,1:T(8,128)S(1)} %get-tuple-element.12, f32[2,1024]{1,0:T(2,128)S(1)} %get-tuple-element.15, f32[1024,256]{0,1:T(8,128)S(1)} %get-tuple-element.11, ...), kind=kOutput, calls=%fused_computation.5 | convolution fusion | flops 2691039232 | bytes 13930496 | tf_op jit(solution)/shard_map/tg,lgn->tln/dot_general | solution.py:73
  358.4 25.4 %all_to_all.10 = bf16[16,160,256]{2,1,0:T(8,128)(2,1)S(1)} all-to-all(bf16[16,160,256]{2,1,0:T(8,128)(2,1)S(1)} %bitcast.66), channel_id=1, replica_groups=mesh['kring'=8,'band'=16] {'band'}, dimensions={0} | all-to-all | bytes 2621440 | tf_op jit(solution)/shard_map/all_to_all | solution.py:80
  383.8 7.5 %gather_fusion.1 = bf16[2048,256]{1,0:T(8,128)(2,1)S(1)} fusion(bf16[2560,256]{1,0:T(8,128)(2,1)S(1)} %bitcast.64, s32[2048]{0:T(1024)S(1)} %get-tuple-element.7), kind=kCustom, calls=%fused_computation.1 | custom fusion | bytes 2105344 | tf_op jit(solution)/shard_map/gather | solution.py:87
  391.4 2.1 fusion.18
  393.5 63.6 %all-reduce.1 = (f32[256]{0:T(256)S(1)}, f32[256]{0:T(256)S(1)}) all-reduce(f32[256]{0:T(256)S(1)} %get-tuple-element.4, f32[256]{0:T(256)S(1)} %get-tuple-element.3), channel_id=1, replica_groups=mesh['kring'=8,'band'=16] {'kring','band'}, use_global_device_ids=true, to_apply=%region_9.10 | all-reduce | flops 512 | bytes 4096 | tf_op jit(solution)/shard_map/psum | solution.py:92
  457.1 0.8 multiply_reduce_fusion
  457.9 62.7 %psum.39 = f32[256]{0:T(256)S(1)} all-reduce(f32[256]{0:T(256)S(1)} %multiply_reduce_fusion), channel_id=1, replica_groups=mesh['kring'=8,'band'=16] {'kring','band'}, use_global_device_ids=true, to_apply=%region_13.14 | all-reduce | flops 256 | bytes 2048 | tf_op jit(solution)/shard_map/psum | solution.py:98
  520.6 1.7 divide_convert_fusion
  (44 shorter events, 5.2 us)
Async XLA Ops:
  13.1 21.9 %copy-start.4 = (s32[2560]{0:T(1024)S(1)}, s32[2560]{0:T(1024)}, u32[]{:S(2)}) copy-start(s32[2560]{0:T(1024)} %param.15) | copy-start | bytes 30724
  13.2 21.9 %copy-start.3 = (f32[2,2,1024]{2,1,0:T(2,128)S(1)}, f32[2,2,1024]{2,1,0:T(2,128)}, u32[]{:S(2)}) copy-start(f32[2,2,1024]{2,1,0:T(2,128)} %param.20) | copy-start | bytes 49156
  13.2 22.0 %copy-start.8 = (u32[128]{0:T(128)S(1)}, u32[128]{0:T(128)}, u32[]{:S(2)}) copy-start(u32[128]{0:T(128)} %constant.62) | copy-start | bytes 1540
  25.5 30.7 %all-to-all-start = ((bf16[16,160,256]{2,1,0:T(8,128)(2,1)}), bf16[16,160,256]{2,1,0:T(8,128)(2,1)S(1)}, u32[]{:S(2)}, u32[]{:S(2)}) async-start(bf16[16,160,256]{2,1,0:T(8,128)(2,1)} %bitcast.2), calls=%async_computation | async-start | bytes 2621440 | tf_op jit(solution)/shard_map/all_to_all | solution.py:37
  34.8 314.4 %all-reduce.6.cloned.1.call-start = ((), (), s32[]{:S(2)}) async-start(), calls=%async_computation.2 | async-start | bytes 4194304 | tf_op jit(solution)/shard_map/psum | solution.py:57
  152.0 29.4 %slice-start = ((s8[5242880]{0:T(1024)(128)(4,1)}), s8[4194304]{0:T(1024)(128)(4,1)S(1)}, s32[]{:S(2)}) async-start(s8[5242880]{0:T(1024)(128)(4,1)} %bitcast.71), calls=%async_computation.3 | async-start | bytes 8388608
  177.1 4.3 slice-start.1
  383.8 7.5 %copy-start = (bf16[2048,256]{1,0:T(8,128)(2,1)S(1)}, bf16[2048,256]{1,0:T(8,128)(2,1)}, u32[]{:S(2)}) copy-start(bf16[2048,256]{1,0:T(8,128)(2,1)} %param.11) | copy-start | bytes 3145732
  383.8 7.5 %copy-start.2 = (f32[2048]{0:T(1024)S(1)}, f32[2048]{0:T(1024)}, u32[]{:S(2)}) copy-start(f32[2048]{0:T(1024)} %param.13) | copy-start | bytes 24580
  383.8 7.5 %copy-start.5 = (f32[256]{0:T(256)S(1)}, f32[256]{0:T(256)}, u32[]{:S(2)}) copy-start(f32[256]{0:T(256)} %param.21) | copy-start | bytes 3076
  391.4 65.7 %copy-start.1 = (bf16[2048,256]{1,0:T(8,128)(2,1)S(1)}, bf16[2048,256]{1,0:T(8,128)(2,1)}, u32[]{:S(2)}) copy-start(bf16[2048,256]{1,0:T(8,128)(2,1)} %param.12) | copy-start | bytes 3145732
  457.1 65.3 %copy-start.6 = (f32[256]{0:T(256)}, f32[256]{0:T(256)S(1)}, u32[]{:S(2)}) copy-start(f32[256]{0:T(256)S(1)} %div.17) | copy-start | bytes 3076
  520.6 1.8 copy-start.7
Sparse Core Ops, SparseCore 0:
  185.9 163.2 all-reduce.5
where the time goes:
time: 530 us; the launch traced here: 529 us
  blocking collectives  353 us (67%)
  waiting for transfers between devices  64.9 us (12%)
  local copies, waits for them, and re-layouts  38.2 us (7%)
  matrix products  29.5 us (6%)
  other arithmetic  19.5 us (4%)
  between operations  14.9 us (3%)
  starting transfers between devices  9.51 us (2%)
    psum x1, blocking collectives, per_device(): direct = lax.psum(direct_part, 'band').astype(jnp.bfloat16)  91.2 us
    unnamed x1, blocking collectives  84.6 us
    psum x1, waiting for transfers between devices, per_device(): exchange_total = lax.psum(exchange_part, ('kring', 'band'))  64.9 us
    psum x1, blocking collectives, per_device(): lax.psum((jnp.sum(current_wide * start_vec, axis=0), jnp.sum(current_wide...  63.6 us
    psum x1, blocking collectives, per_device(): lax.psum(jnp.sum(residual * residual, axis=0), ('kring', 'band'))  62.7 us
    all_to_all x1, blocking collectives, per_device(): lax.all_to_all(kernel_rows.reshape(band_count, capacity, chains), 'band',...  25.4 us
    all_gather x1, blocking collectives, per_device(): pieces = lax.all_gather(projected[None], 'kring', axis=0, tiled=True)  25.1 us
    gather x1, local copies, waits for them, and re-layouts, per_device(): blocks = jnp.take(screened, distance, axis=0)  12 us
  transfers between devices with their start and end apart: 2, of which 1 were waited for; matrix products, arithmetic and copies ran while one was open for 5% of the time, Pallas kernels for 0%

commit v1 on v0

--- a/solution.py
+++ b/solution.py
@@ -66,7 +66,7 @@
     distance = jnp.mod(group_index - jnp.arange(number, dtype=jnp.int32), group_count)
     blocks = jnp.take(screened, distance, axis=0)
     direct_part = jnp.einsum("kaphg,kapn->hgn", blocks, pieces, preferred_element_type=jnp.float32)
-    direct = lax.psum(direct_part, "band").astype(jnp.bfloat16)
+    direct = jnp.sum(lax.all_gather(direct_part, "band"), axis=0).astype(jnp.bfloat16)
     both_direct = jnp.einsum(
         "tg,lgn->tln", conduction_pairs, direct, preferred_element_type=jnp.float32
     )

time: 530 us -> 578 us (1.091)
  waiting for transfers between devices: 64.9 us -> 189 us
  blocking collectives: 353 us -> 260 us
  other arithmetic: 19.5 us -> 31.7 us
    all_gather x0 -> x1, waiting for transfers between devices: none -> 118 us  [per_device(): lax.all_gather(direct_part, 'band')]
    psum x1 -> x0, blocking collectives: 91.2 us -> none  [per_device(): direct = lax.psum(direct_part, 'band').astype(jnp.bfloat16)]
    reduce_sum x0 -> x1, other arithmetic: none -> 12.2 us  [per_device(): jnp.sum(lax.all_gather(direct_part, 'band'), axis=0).astype(jnp.bfloat16)]
  transfers between devices with their start and end apart: 2 -> 3, of which waited for: 1 -> 2; matrix products, arithmetic and copies ran while one was open for 5% -> 5% of each run, Pallas kernels for 0% -> 0%
where the time goes in v1:
time: 578 us; the launch traced here: 577 us
  blocking collectives  260 us (45%)
  waiting for transfers between devices  189 us (33%)
  local copies, waits for them, and re-layouts  40.1 us (7%)
  other arithmetic  31.7 us (5%)
  matrix products  30.1 us (5%)
  between operations  16.4 us (3%)
  starting transfers between devices  9.55 us (2%)
    all_gather x1, waiting for transfers between devices, per_device(): lax.all_gather(direct_part, 'band')  118 us
    unnamed x1, blocking collectives  85.9 us
    psum x1, waiting for transfers between devices, per_device(): exchange_total = lax.psum(exchange_part, ('kring', 'band'))  70.3 us
    psum x1, blocking collectives, per_device(): lax.psum((jnp.sum(current_wide * start_vec, axis=0), jnp.sum(current_wide...  64.5 us
    psum x1, blocking collectives, per_device(): lax.psum(jnp.sum(residual * residual, axis=0), ('kring', 'band'))  62.9 us
    all_gather x1, blocking collectives, per_device(): pieces = lax.all_gather(projected[None], 'kring', axis=0, tiled=True)  24.6 us
    all_to_all x1, blocking collectives, per_device(): lax.all_to_all(kernel_rows.reshape(band_count, capacity, chains), 'band',...  22.6 us
    reduce_sum x1, other arithmetic, per_device(): jnp.sum(lax.all_gather(direct_part, 'band'), axis=0).astype(jnp.bfloat16)  12.2 us
  transfers between devices with their start and end apart: 3, of which 2 were waited for; matrix products, arithmetic and copies ran while one was open for 5% of the time, Pallas kernels for 0%

profile of v1, /device:TPU:1, one launch (start us, length us, event | category | flops | bytes accessed | tf_op | source)
XLA Modules:
  0.0 577.0 jit_solution(11137458029160039414)
XLA Ops:
  8.7 4.5 reduce-window.6
  15.5 10.8 %scatter_custom_fusion = bf16[2560,256]{1,0:T(8,128)(2,1)} fusion(s32[2048]{0:T(1024)S(1)} %get-tuple-element.8, bf16[2048,256]{1,0:T(8,128)(2,1)} %param.11, bf16[]{:T(256)} %constant.46.clone.1), kind=kCustom, calls=%fused_computation.44 | custom fusion | bytes 1311232 | tf_op jit(solution)/shard_map/scatter | solution.py:36
  26.3 9.3 %all-to-all-start = ((bf16[16,160,256]{2,1,0:T(8,128)(2,1)}), bf16[16,160,256]{2,1,0:T(8,128)(2,1)S(1)}, u32[]{:S(2)}, u32[]{:S(2)}) async-start(bf16[16,160,256]{2,1,0:T(8,128)(2,1)} %bitcast.2), calls=%async_computation | async-start | bytes 2621440 | tf_op jit(solution)/shard_map/all_to_all | solution.py:37
  37.1 12.0 %gather_fusion = bf16[8,2,64,2,1024]{4,3,2,1,0:T(2,128)(2,1)} fusion(bf16[8,2,64,2,1024]{4,3,2,1,0:T(2,128)(2,1)} %param.19, s32[1024]{0:T(1024)S(1)} %pad_clamp_fusion), kind=kCustom, calls=%fused_computation | custom fusion | bytes 8388640 | tf_op jit(solution)/shard_map/jit(_take)/gather | solution.py:67
  49.2 7.8 %broadcast_select_fusion = bf16[8,2,64,2,1024]{4,3,2,1,0:T(2,128)(2,1)} fusion(bf16[8,2,64,2,1024]{4,3,2,1,0:T(2,128)(2,1)} %gather_fusion, pred[8]{0:T(512)(128)(4,1)S(1)} %compare_and_fusion), kind=kLoop, calls=%fused_computation.3 | loop fusion | flops 2097152 | bytes 8388616 | tf_op jit(solution)/shard_map/jit(_take)/select_n | solution.py:67
  57.7 6.7 %fusion.28 = f32[2,1024,256]{1,2,0:T(8,128)} fusion(bf16[2560,1024]{1,0:T(8,128)(2,1)} %param.17, bf16[2560,2]{0,1:T(2,128)(2,1)S(1)} %get-tuple-element.10, bf16[2560,256]{0,1:T(8,128)(2,1)S(1)} %copy.25), kind=kOutput, calls=%fused_computation.32 | convolution fusion | flops 2685665280 | bytes 8660992 | tf_op jit(solution)/shard_map/tg,tln->lgn/dot_general | solution.py:48
  64.4 2.8 copy.26
  67.3 6.7 %fusion.23 = f32[2,1024,256]{1,2,0:T(8,128)} fusion(bf16[2560,1024]{1,0:T(8,128)(2,1)} %param.18, bf16[2560,2]{0,1:T(2,128)(2,1)S(1)} %get-tuple-element.10, bf16[2560,256]{0,1:T(8,128)(2,1)S(1)} %copy.25), kind=kOutput, calls=%fused_computation.31 | convolution fusion | flops 2685665280 | bytes 8660992 | tf_op jit(solution)/shard_map/tg,tln->lgn/dot_general | solution.py:51
  74.0 85.9 %all-reduce.6 = bf16[2,1024,256]{2,0,1:T(2,128)(2,1)S(1)} all-reduce(f32[2,1024,256]{2,0,1:T(2,128)S(1)} %copy.26), channel_id=4, replica_groups=mesh['kring'=8,'band'=16] {'band'}, use_global_device_ids=true, to_apply=%region_5.6.clone | all-reduce | flops 524288 | bytes 3145728
  159.9 24.6 %all-gather = bf16[16,64,256]{2,1,0:T(8,128)(2,1)S(1)} all-gather(bf16[2,64,256]{2,1,0:T(8,128)(2,1)S(1)} %copy.27), channel_id=2, replica_groups=mesh['kring'=8,'band'=16] {'kring'}, dimensions={0}, use_global_device_ids=true | all-gather | bytes 589824 | tf_op jit(solution)/shard_map/all_gather | solution.py:64
  184.5 5.6 fusion.20
  190.9 70.3 %all-reduce.5.cloned.1.call-done = f32[2,1024,256]{1,2,0:T(8,128)} async-done(((f32[2,1024,256]{1,2,0:T(8,128)}), f32[2,1024,256]{1,2,0:T(8,128)}) %all-reduce.5.cloned.1.call-update) | async-done | bytes 2097168 | tf_op jit(solution)/shard_map/psum | solution.py:57
  261.2 3.7 slice_bitcast_fusion.1
  264.9 118.3 %all-gather.4.cloned.1.call-done = f32[32,1024,256]{2,1,0:T(8,128)} async-done(((f32[2,1024,256]{2,1,0:T(8,128)}), f32[32,1024,256]{2,1,0:T(8,128)}) %all-gather.4.cloned.1.call-update) | async-done | bytes 33554448 | tf_op jit(solution)/shard_map/all_gather | solution.py:69
  383.2 12.2 %reduce_sum.55 = bf16[2,1024,256]{2,1,0:T(8,128)(2,1)S(1)} reduce(f32[16,2,1024,256]{3,2,1,0:T(8,128)} %bitcast.66, f32[]{:T(128)} %constant.57.clone.1), dimensions={0}, to_apply=%region_6.7 | reduce | flops 7864320 | bytes 34603012 | tf_op jit(solution)/shard_map/reduce_sum | solution.py:69
  395.5 5.1 fusion.1
  400.5 6.1 %fusion = bf16[2560,256]{0,1:T(8,128)(2,1)S(1)} fusion(f32[2,256,2560]{2,1,0:T(8,128)S(1)} %fusion.1, bf16[2560,1024]{1,0:T(8,128)(2,1)} %param.18, f32[2560,2]{0,1:T(2,128)S(1)} %get-tuple-element.9, f32[1024,256]{0,1:T(8,128)S(1)} %copy-done.3, f32[2,1024]{1,0:T(2,128)S(1)} %get-tuple-element.15, f32[1024,256]{0,1:T(8,128)S(1)} %copy-done.2, ...), kind=kOutput, calls=%fused_computation.5 | convolution fusion | flops 2691039232 | bytes 13930496 | tf_op jit(solution)/shard_map/tg,lgn->tln/dot_general | solution.py:73
  407.3 22.6 %all_to_all.10 = bf16[16,160,256]{2,1,0:T(8,128)(2,1)S(1)} all-to-all(bf16[16,160,256]{2,1,0:T(8,128)(2,1)S(1)} %bitcast.68), channel_id=1, replica_groups=mesh['kring'=8,'band'=16] {'band'}, dimensions={0} | all-to-all | bytes 2621440 | tf_op jit(solution)/shard_map/all_to_all | solution.py:80
  429.9 7.5 %gather_fusion.1 = bf16[2048,256]{1,0:T(8,128)(2,1)S(1)} fusion(bf16[2560,256]{1,0:T(8,128)(2,1)S(1)} %bitcast.65, s32[2048]{0:T(1024)S(1)} %get-tuple-element.7), kind=kCustom, calls=%fused_computation.1 | custom fusion | bytes 2105344 | tf_op jit(solution)/shard_map/gather | solution.py:87
  437.5 2.1 fusion.18
  439.6 64.5 %all-reduce.1 = (f32[256]{0:T(256)S(1)}, f32[256]{0:T(256)S(1)}) all-reduce(f32[256]{0:T(256)S(1)} %get-tuple-element.4, f32[256]{0:T(256)S(1)} %get-tuple-element.3), channel_id=1, replica_groups=mesh['kring'=8,'band'=16] {'kring','band'}, use_global_device_ids=true, to_apply=%region_9.10 | all-reduce | flops 512 | bytes 4096 | tf_op jit(solution)/shard_map/psum | solution.py:92
  504.1 0.8 multiply_reduce_fusion
  504.9 62.9 %psum.31 = f32[256]{0:T(256)S(1)} all-reduce(f32[256]{0:T(256)S(1)} %multiply_reduce_fusion), channel_id=1, replica_groups=mesh['kring'=8,'band'=16] {'kring','band'}, use_global_device_ids=true, to_apply=%region_13.14 | all-reduce | flops 256 | bytes 2048 | tf_op jit(solution)/shard_map/psum | solution.py:98
  567.8 1.7 divide_convert_fusion
  (46 shorter events, 6.0 us)
Async XLA Ops:
  14.0 21.8 %copy-start.6 = (s32[2560]{0:T(1024)S(1)}, s32[2560]{0:T(1024)}, u32[]{:S(2)}) copy-start(s32[2560]{0:T(1024)} %param.15) | copy-start | bytes 30724
  14.0 21.9 %copy-start.10 = (u32[128]{0:T(128)S(1)}, u32[128]{0:T(128)}, u32[]{:S(2)}) copy-start(u32[128]{0:T(128)} %constant.62) | copy-start | bytes 1540
  26.3 30.7 %all-to-all-start = ((bf16[16,160,256]{2,1,0:T(8,128)(2,1)}), bf16[16,160,256]{2,1,0:T(8,128)(2,1)S(1)}, u32[]{:S(2)}, u32[]{:S(2)}) async-start(bf16[16,160,256]{2,1,0:T(8,128)(2,1)} %bitcast.2), calls=%async_computation | async-start | bytes 2621440 | tf_op jit(solution)/shard_map/all_to_all | solution.py:37
  35.6 225.6 %all-reduce.5.cloned.1.call-start = ((), (), s32[]{:S(2)}) async-start(), calls=%async_computation.2 | async-start | bytes 4194304 | tf_op jit(solution)/shard_map/psum | solution.py:57
  73.9 309.3 %all-gather.4.cloned.1.call-start = ((), (), s32[]{:S(2)}) async-start(), calls=%async_computation.3 | async-start | bytes 35651584 | tf_op jit(solution)/shard_map/all_gather | solution.py:69
  190.1 0.7 copy-start.5
  395.4 5.1 copy-start.2
  395.4 5.1 copy-start.3
  429.9 7.5 %copy-start = (bf16[2048,256]{1,0:T(8,128)(2,1)S(1)}, bf16[2048,256]{1,0:T(8,128)(2,1)}, u32[]{:S(2)}) copy-start(bf16[2048,256]{1,0:T(8,128)(2,1)} %param.11) | copy-start | bytes 3145732
  429.9 7.5 %copy-start.4 = (f32[2048]{0:T(1024)S(1)}, f32[2048]{0:T(1024)}, u32[]{:S(2)}) copy-start(f32[2048]{0:T(1024)} %param.13) | copy-start | bytes 24580
  429.9 7.5 %copy-start.7 = (f32[256]{0:T(256)S(1)}, f32[256]{0:T(256)}, u32[]{:S(2)}) copy-start(f32[256]{0:T(256)} %param.21) | copy-start | bytes 3076
  437.4 66.6 %copy-start.1 = (bf16[2048,256]{1,0:T(8,128)(2,1)S(1)}, bf16[2048,256]{1,0:T(8,128)(2,1)}, u32[]{:S(2)}) copy-start(bf16[2048,256]{1,0:T(8,128)(2,1)} %param.12) | copy-start | bytes 3145732
  504.1 65.5 %copy-start.8 = (f32[256]{0:T(256)}, f32[256]{0:T(256)S(1)}, u32[]{:S(2)}) copy-start(f32[256]{0:T(256)S(1)} %div.17) | copy-start | bytes 3076
  567.8 1.8 copy-start.9
Sparse Core Ops, SparseCore 0:
  74.1 187.0 all-reduce.4
Sparse Core Ops, SparseCore 1:
  190.3 192.9 all-gather.3
